TPU v7x, 32 devices: a whole 2x2x4 slice. The times are simulated.
32 devices in a mesh: ha: 2 (over y), wa: 16 (over z, x, core).
Axes of the slice: x: 2, y: 2, z: 4, core: 2. Of those that a mesh axis runs over, the one named last changes fastest.
Arguments:
- block_input: bfloat16 [3, 46, 160, 128], P(None, 'ha', 'wa'), may hold values from -6 to 6
- cotangent: bfloat16 [3, 46, 160, 128], P(None, 'ha', 'wa'), may hold values from -6 to 6
- kernel_one: bfloat16 [3, 3, 3, 128, 128], replicated, may hold values from -0.109375 to 0.109375
- bias_one: float32 [128], replicated, may hold values from -3 to 3
- kernel_two: bfloat16 [3, 3, 3, 128, 128], replicated, may hold values from -0.109375 to 0.109375
- scale_one: float32 [128], replicated, may hold values from 0.5 to 2
- shift_one: float32 [128], replicated, may hold values from -1 to 1
- scale_two: float32 [128], replicated, may hold values from 0.5 to 2
- shift_two: float32 [128], replicated, may hold values from -1 to 1
Outputs:
- grad_input: bfloat16 [3, 46, 160, 128], P(None, 'ha', 'wa')
- grad_kernel_one: float32 [3, 3, 3, 128, 128], replicated
- grad_bias_one: float32 [128], replicated
- grad_kernel_two: float32 [3, 3, 3, 128, 128], replicated
- grad_bias_two: float32 [128], replicated
All inputs are finite; a program needn't handle non-finite values.
Results may differ from a plain program's by a relative error of at most 0.0054.
Values may be sent and summed in bfloat16 or wider, within the bound.
A program may use at most 64 MiB of HBM per device.

v0:
```python
import math
import jax
import jax.numpy as jnp
from jax import lax
from jax.sharding import PartitionSpec as P


def with_halo(cells, sides, width):
    for axis, dim in sides:
        count = lax.axis_size(axis)
        ends = count - 1
        head = lax.slice_in_dim(cells, 0, width, axis=dim)
        tail = lax.slice_in_dim(cells, cells.shape[dim] - width, cells.shape[dim], axis=dim)
        cells = jnp.concatenate(
            [
                lax.ppermute(tail, axis, [(i, (i + 1) % count) for i in range(ends)]),
                cells,
                lax.ppermute(head, axis, [((i + 1) % count, i) for i in range(ends)]),
            ],
            axis=dim,
        )
    return cells


def slope(value):
    sigma = jax.nn.sigmoid(value)
    return sigma * (1.0 + value * (1.0 - sigma))


def widen(padded, columns):
    return jnp.concatenate([padded[:, :, shift : shift + columns] for shift in range(3)], axis=-1)


def convolve(wide, kernel, frames, rows):
    columns = wide.shape[2]
    inner = kernel.shape[3]
    total = jnp.zeros((frames * rows * columns, kernel.shape[4]), jnp.float32)
    for step_t in range(3):
        for step_h in range(3):
            slab = wide[step_t : step_t + frames, step_h : step_h + rows].reshape(-1, 3 * inner)
            total = total + jnp.dot(
                slab,
                kernel[step_t, step_h].reshape(3 * inner, -1),
                preferred_element_type=jnp.float32,
            )
    return total.reshape(frames, rows, columns, -1)


def kernel_terms(wide, grads, frames, rows):
    inner = wide.shape[3] // 3
    pieces = []
    for step_t in range(3):
        for step_h in range(3):
            slab = wide[step_t : step_t + frames, step_h : step_h + rows].reshape(-1, 3 * inner)
            pieces.append(
                lax.dot_general(
                    slab, grads, (((0,), (0,)), ((), ())), preferred_element_type=jnp.float32
                )
            )
    return jnp.stack(pieces).reshape(3, 3, 3, inner, grads.shape[1])


def flipped(kernel):
    return jnp.transpose(kernel[::-1, ::-1, ::-1], (0, 1, 2, 4, 3))


def body(
    block_input,
    cotangent,
    kernel_one,
    bias_one,
    kernel_two,
    scale_one,
    shift_one,
    scale_two,
    shift_two,
):
    frames, rows, columns, chans = block_input.shape
    factor = 1.0 / math.sqrt(frames * rows * lax.axis_size("ha") * columns * lax.axis_size("wa"))
    front = ((2, 0), (0, 0), (0, 0), (0, 0))
    back = ((0, 2), (0, 0), (0, 0), (0, 0))
    first_pre = block_input.astype(jnp.float32) * scale_one + shift_one
    first_act = jax.nn.silu(first_pre).astype(jnp.bfloat16)
    joined = with_halo(jnp.stack([first_act, cotangent]), (("ha", 2), ("wa", 3)), 1)
    first_rim = joined[0]
    cot_halo = joined[1]
    first_wide = widen(jnp.pad(first_rim, front), columns)
    hidden = convolve(first_wide, kernel_one, frames, rows) + bias_one
    second_pre = hidden * scale_two + shift_two
    second_act = jax.nn.silu(second_pre).astype(jnp.bfloat16)
    second_rim = with_halo(second_act, (("ha", 1), ("wa", 2)), 1)
    second_wide = widen(jnp.pad(second_rim, front), columns)
    upstream = cotangent.reshape(-1, chans)
    grad_two = kernel_terms(second_wide, upstream, frames, rows)
    bias_b = jnp.sum(cotangent.astype(jnp.float32), axis=(0, 1, 2))
    cot_wide = widen(jnp.pad(cot_halo, back), columns)
    back_two = convolve(cot_wide, flipped(kernel_two), frames, rows)
    inner = (back_two * slope(second_pre) * scale_two).astype(jnp.bfloat16)
    inner_rim = with_halo(inner, (("ha", 1), ("wa", 2)), 1)
    inner_wide = widen(jnp.pad(inner_rim, back), columns)
    back_one = convolve(inner_wide, flipped(kernel_one), frames, rows)
    grad_input = (cotangent.astype(jnp.float32) + back_one * slope(first_pre) * scale_one).astype(
        jnp.bfloat16
    )
    grad_one = kernel_terms(first_wide, inner.reshape(-1, chans), frames, rows)
    bias_a = jnp.sum(inner.astype(jnp.float32), axis=(0, 1, 2))
    grad_one, bias_a, grad_two, bias_b = lax.psum(
        (grad_one, bias_a, grad_two, bias_b), ("ha", "wa")
    )
    return (grad_input, grad_one * factor, bias_a * factor, grad_two * factor, bias_b * factor)


def solution(mesh):
    return jax.shard_map(
        body,
        mesh=mesh,
        in_specs=(
            P(None, "ha", "wa", None),
            P(None, "ha", "wa", None),
            P(),
            P(),
            P(),
            P(),
            P(),
            P(),
            P(),
        ),
        out_specs=(P(None, "ha", "wa", None), P(), P(), P(), P()),
        check_vma=False,
    )
```

profile of v0, /device:TPU:0, one launch (start us, length us, event | category | flops | bytes accessed | tf_op | source)
XLA Modules:
  0.0 281.3 jit_solution(7883911846606421409)
XLA Ops:
  9.3 4.9 %collective-permute-start = (bf16[2,3,1,10,128]{4,2,3,1,0:T(2,128)(2,1)S(1)}, bf16[2,3,1,10,128]{4,2,3,1,0:T(2,128)(2,1)S(1)}, u32[]{:S(2)}, u32[]{:S(2)}) collective-permute-start(bf16[2,3,1,10,128]{4,2,3,1,0:T(2,128)(2,1)S(1)} %get-tuple-element.75), channel_id=1, source_target_pairs={{0,16},{1,17},{2,18},{3,19},{4,20},{5,21},{6,22},{7,23},{8,24},{9,... | collective-permute-start | bytes 46088 | tf_op jit(solution)/shard_map/ppermute | solution.py:16
  14.2 1.3 collective-permute-start.1
  15.5 2.2 fusion.65
  17.7 1.4 copy.39
  19.0 2.0 copy.18
  22.3 1.5 collective-permute-start.2
  23.7 1.3 collective-permute-start.3
  26.0 2.5 collective-permute-done.3
  28.7 1.3 pad_slice_fusion.2
  30.2 1.9 fusion.63
  45.3 1.4 pad_maximum_fusion.1
  46.6 2.3 fusion.62
  67.6 1.3 fusion.72
  69.0 1.3 convolution_add_fusion.15
  73.3 1.3 fusion.71
  74.6 1.5 convolution_add_fusion.23
  79.6 4.5 %collective-permute-start.4 = (bf16[3,1,10,128]{3,1,2,0:T(2,128)(2,1)S(1)}, bf16[3,1,10,128]{3,1,2,0:T(2,128)(2,1)S(1)}, u32[]{:S(2)}, u32[]{:S(2)}) collective-permute-start(bf16[3,1,10,128]{3,1,2,0:T(2,128)(2,1)S(1)} %get-tuple-element.91), channel_id=1, source_target_pairs={{0,16},{1,17},{2,18},{3,19},{4,20},{5,21},{6,22},{7,23},{8,24},{9,... | collective-permute-start | bytes 23048 | tf_op jit(solution)/shard_map/ppermute | solution.py:16
  84.1 1.3 collective-permute-start.5
  85.5 4.5 %collective-permute-start.8 = (bf16[3,1,10,128]{3,1,2,0:T(2,128)(2,1)S(1)}, bf16[3,1,10,128]{3,1,2,0:T(2,128)(2,1)S(1)}, u32[]{:S(2)}, u32[]{:S(2)}) collective-permute-start(bf16[3,1,10,128]{3,1,2,0:T(2,128)(2,1)S(1)} %get-tuple-element.89), channel_id=1, source_target_pairs={{0,16},{1,17},{2,18},{3,19},{4,20},{5,21},{6,22},{7,23},{8,24},{9,... | collective-permute-start | bytes 23048 | tf_op jit(solution)/shard_map/ppermute | solution.py:16
  90.0 1.3 collective-permute-start.9
  94.3 3.9 %collective-permute-start.6 = (bf16[3,25,1,128]{3,1,2,0:T(8,128)(2,1)S(1)}, bf16[3,25,1,128]{3,1,2,0:T(8,128)(2,1)S(1)}, u32[]{:S(2)}, u32[]{:S(2)}) collective-permute-start(bf16[3,25,1,128]{3,1,2,0:T(8,128)(2,1)S(1)} %get-tuple-element.85), channel_id=1, source_target_pairs={{0,1},{1,2},{2,3},{3,4},{4,5},{5,6},{6,7},{7,8},{8,9},{9,10},{10,1... | collective-permute-start | bytes 57608 | tf_op jit(solution)/shard_map/ppermute | solution.py:16
  98.2 1.3 collective-permute-start.7
  100.2 3.9 %collective-permute-start.10 = (bf16[3,25,1,128]{3,1,2,0:T(8,128)(2,1)}, bf16[3,25,1,128]{3,1,2,0:T(8,128)(2,1)}, u32[]{:S(2)}, u32[]{:S(2)}) collective-permute-start(bf16[3,25,1,128]{3,1,2,0:T(8,128)(2,1)} %get-tuple-element.83), channel_id=1, source_target_pairs={{0,1},{1,2},{2,3},{3,4},{4,5},{5,6},{6,7},{7,8},{8,9},{9,10},{10,1... | collective-permute-start | bytes 57608 | tf_op jit(solution)/shard_map/ppermute | solution.py:16
  104.1 1.3 collective-permute-start.11
  106.0 1.9 fusion.61
  125.2 1.4 convolution_add_fusion.7
  126.6 1.2 convolution_add_fusion.6
  132.3 1.4 convolution_add_fusion.3
  135.9 45.0 %all-reduce.4 = (f32[128]{0:T(128)S(1)}, f32[128]{0:T(128)S(1)}) all-reduce(f32[128]{0:T(128)S(1)} %get-tuple-element.93, f32[128]{0:T(128)S(1)} %get-tuple-element.87), channel_id=1, replica_groups=mesh['ha'=2,'wa'=16] {'ha','wa'}, use_global_device_ids=true, to_apply=%region_2.3 | all-reduce | flops 256 | bytes 2048 | tf_op jit(solution)/shard_map/psum | solution.py:107
  181.9 88.1 %all-reduce.8.cloned.1.call-done = (f32[3,3,3,128,128]{4,3,2,1,0:T(8,128)}, f32[3,3,3,128,128]{4,3,2,1,0:T(8,128)}) async-done(((f32[3,3,3,128,128]{4,3,2,1,0:T(8,128)}, f32[3,3,3,128,128]{4,3,2,1,0:T(8,128)}), (f32[3,3,3,128,128]{4,3,2,1,0:T(8,128)}, f32[3,3,3,128,128]{4,3,2,1,0:T(8,128)})) %all-reduce.8.cloned.1.call-update) | async-done | bytes 3538960 | tf_op jit(solution)/shard_map/psum | solution.py:107
  270.0 3.1 %broadcast_multiply_fusion = f32[3,3,3,128,128]{4,3,2,1,0:T(8,128)} fusion(f32[3,3,3,128,128]{4,3,2,1,0:T(8,128)} %get-tuple-element.8), kind=kLoop, calls=%fused_computation.76 | loop fusion | flops 442368 | bytes 3538944 | tf_op jit(solution)/shard_map/mul | solution.py:110
  273.1 1.4 broadcast_multiply_fusion.1
  (248 shorter events, 71.2 us)
Async XLA Ops:
  7.2 10.5 %copy-start = (bf16[3,3,3,128,128]{4,3,2,1,0:T(8,128)(2,1)S(1)}, bf16[3,3,3,128,128]{4,3,2,1,0:T(8,128)(2,1)}, u32[]{:S(2)}) copy-start(bf16[3,3,3,128,128]{4,3,2,1,0:T(8,128)(2,1)} %param.11) | copy-start | bytes 2654212
  7.2 262.8 %all-reduce.8.cloned.1.call-start = ((), (), s32[]{:S(2)}) async-start(), calls=%async_computation | async-start | bytes 7077888 | tf_op jit(solution)/shard_map/psum | solution.py:107
  9.3 12.9 %collective-permute-start = (bf16[2,3,1,10,128]{4,2,3,1,0:T(2,128)(2,1)S(1)}, bf16[2,3,1,10,128]{4,2,3,1,0:T(2,128)(2,1)S(1)}, u32[]{:S(2)}, u32[]{:S(2)}) collective-permute-start(bf16[2,3,1,10,128]{4,2,3,1,0:T(2,128)(2,1)S(1)} %get-tuple-element.75), channel_id=1, source_target_pairs={{0,16},{1,17},{2,18},{3,19},{4,20},{5,21},{6,22},{7,23},{8,24},{9,... | collective-permute-start | bytes 46088 | tf_op jit(solution)/shard_map/ppermute | solution.py:16
  14.2 8.0 %collective-permute-start.1 = (bf16[2,3,1,10,128]{4,2,3,1,0:T(2,128)(2,1)S(1)}, bf16[2,3,1,10,128]{4,2,3,1,0:T(2,128)(2,1)S(1)}, u32[]{:S(2)}, u32[]{:S(2)}) collective-permute-start(bf16[2,3,1,10,128]{4,2,3,1,0:T(2,128)(2,1)S(1)} %get-tuple-element.76), channel_id=1, source_target_pairs={{16,0},{17,1},{18,2},{19,3},{20,4},{21,5},{22,6},{23,7},{24,8},{25... | collective-permute-start | bytes 46088 | tf_op jit(solution)/shard_map/ppermute | solution.py:18
  22.3 3.7 %collective-permute-start.2 = (bf16[2,3,25,1,128]{4,2,3,1,0:T(8,128)(2,1)S(1)}, bf16[2,3,25,1,128]{4,2,3,1,0:T(8,128)(2,1)S(1)}, u32[]{:S(2)}, u32[]{:S(2)}) collective-permute-start(bf16[2,3,25,1,128]{4,2,3,1,0:T(8,128)(2,1)S(1)} %get-tuple-element.73), channel_id=1, source_target_pairs={{0,1},{1,2},{2,3},{3,4},{4,5},{5,6},{6,7},{7,8},{8,9},{9,10},{10,1... | collective-permute-start | bytes 115208 | tf_op jit(solution)/shard_map/ppermute | solution.py:16
  23.7 4.7 %collective-permute-start.3 = (bf16[2,3,25,1,128]{4,2,3,1,0:T(8,128)(2,1)S(1)}, bf16[2,3,25,1,128]{4,2,3,1,0:T(8,128)(2,1)S(1)}, u32[]{:S(2)}, u32[]{:S(2)}) collective-permute-start(bf16[2,3,25,1,128]{4,2,3,1,0:T(8,128)(2,1)S(1)} %get-tuple-element.74), channel_id=1, source_target_pairs={{1,0},{2,1},{3,2},{4,3},{5,4},{6,5},{7,6},{8,7},{9,8},{10,9},{11,1... | collective-permute-start | bytes 115208 | tf_op jit(solution)/shard_map/ppermute | solution.py:18
  66.6 2.4 copy-start.16
  67.6 2.7 copy-start.17
  67.6 2.7 copy-start.50
  67.6 3.1 %copy-start.18 = (bf16[690,384]{1,0:T(8,128)(2,1)S(1)}, bf16[690,384]{1,0:T(8,128)(2,1)}, u32[]{:S(2)}) copy-start(bf16[690,384]{1,0:T(8,128)(2,1)} %reshape.144) | copy-start | bytes 1589764
  67.6 3.1 %copy-start.49 = (bf16[1,1,3,128,128]{4,3,2,1,0:T(8,128)(2,1)S(1)}, bf16[1,1,3,128,128]{4,3,2,1,0:T(8,128)(2,1)}, u32[]{:S(2)}) copy-start(bf16[1,1,3,128,128]{4,3,2,1,0:T(8,128)(2,1)} %get-tuple-element.50) | copy-start | bytes 294916
  73.0 3.1 %copy-start.4 = (bf16[690,384]{1,0:T(8,128)(2,1)S(1)}, bf16[690,384]{1,0:T(8,128)(2,1)}, u32[]{:S(2)}) copy-start(bf16[690,384]{1,0:T(8,128)(2,1)} %reshape.133) | copy-start | bytes 1589764
  73.0 3.1 %copy-start.43 = (bf16[1,1,3,128,128]{4,3,2,1,0:T(8,128)(2,1)S(1)}, bf16[1,1,3,128,128]{4,3,2,1,0:T(8,128)(2,1)}, u32[]{:S(2)}) copy-start(bf16[1,1,3,128,128]{4,3,2,1,0:T(8,128)(2,1)} %get-tuple-element.60) | copy-start | bytes 294916
  73.3 3.2 %copy-start.5 = (bf16[690,384]{1,0:T(8,128)(2,1)S(1)}, bf16[690,384]{1,0:T(8,128)(2,1)}, u32[]{:S(2)}) copy-start(bf16[690,384]{1,0:T(8,128)(2,1)} %reshape.134) | copy-start | bytes 1589764
  73.3 3.2 %copy-start.42 = (bf16[1,1,3,128,128]{4,3,2,1,0:T(8,128)(2,1)S(1)}, bf16[1,1,3,128,128]{4,3,2,1,0:T(8,128)(2,1)}, u32[]{:S(2)}) copy-start(bf16[1,1,3,128,128]{4,3,2,1,0:T(8,128)(2,1)} %get-tuple-element.59) | copy-start | bytes 294916
  74.6 2.3 copy-start.6
  79.6 14.7 %collective-permute-start.4 = (bf16[3,1,10,128]{3,1,2,0:T(2,128)(2,1)S(1)}, bf16[3,1,10,128]{3,1,2,0:T(2,128)(2,1)S(1)}, u32[]{:S(2)}, u32[]{:S(2)}) collective-permute-start(bf16[3,1,10,128]{3,1,2,0:T(2,128)(2,1)S(1)} %get-tuple-element.91), channel_id=1, source_target_pairs={{0,16},{1,17},{2,18},{3,19},{4,20},{5,21},{6,22},{7,23},{8,24},{9,... | collective-permute-start | bytes 23048 | tf_op jit(solution)/shard_map/ppermute | solution.py:16
  84.1 10.1 %collective-permute-start.5 = (bf16[3,1,10,128]{3,1,2,0:T(2,128)(2,1)S(1)}, bf16[3,1,10,128]{3,1,2,0:T(2,128)(2,1)S(1)}, u32[]{:S(2)}, u32[]{:S(2)}) collective-permute-start(bf16[3,1,10,128]{3,1,2,0:T(2,128)(2,1)S(1)} %get-tuple-element.92), channel_id=1, source_target_pairs={{16,0},{17,1},{18,2},{19,3},{20,4},{21,5},{22,6},{23,7},{24,8},{25... | collective-permute-start | bytes 23048 | tf_op jit(solution)/shard_map/ppermute | solution.py:18
  85.5 14.0 %collective-permute-start.8 = (bf16[3,1,10,128]{3,1,2,0:T(2,128)(2,1)S(1)}, bf16[3,1,10,128]{3,1,2,0:T(2,128)(2,1)S(1)}, u32[]{:S(2)}, u32[]{:S(2)}) collective-permute-start(bf16[3,1,10,128]{3,1,2,0:T(2,128)(2,1)S(1)} %get-tuple-element.89), channel_id=1, source_target_pairs={{0,16},{1,17},{2,18},{3,19},{4,20},{5,21},{6,22},{7,23},{8,24},{9,... | collective-permute-start | bytes 23048 | tf_op jit(solution)/shard_map/ppermute | solution.py:16
  90.0 9.5 %collective-permute-start.9 = (bf16[3,1,10,128]{3,1,2,0:T(2,128)(2,1)S(1)}, bf16[3,1,10,128]{3,1,2,0:T(2,128)(2,1)S(1)}, u32[]{:S(2)}, u32[]{:S(2)}) collective-permute-start(bf16[3,1,10,128]{3,1,2,0:T(2,128)(2,1)S(1)} %get-tuple-element.90), channel_id=1, source_target_pairs={{16,0},{17,1},{18,2},{19,3},{20,4},{21,5},{22,6},{23,7},{24,8},{25... | collective-permute-start | bytes 23048 | tf_op jit(solution)/shard_map/ppermute | solution.py:18
  94.3 11.1 %copy-start.27 = (f32[9,384,128]{2,1,0:T(8,128)}, f32[9,384,128]{2,1,0:T(8,128)S(1)}, u32[]{:S(2)}) copy-start(f32[9,384,128]{2,1,0:T(8,128)S(1)} %fusion.9) | copy-start | bytes 5308420
  94.3 11.1 %collective-permute-start.6 = (bf16[3,25,1,128]{3,1,2,0:T(8,128)(2,1)S(1)}, bf16[3,25,1,128]{3,1,2,0:T(8,128)(2,1)S(1)}, u32[]{:S(2)}, u32[]{:S(2)}) collective-permute-start(bf16[3,25,1,128]{3,1,2,0:T(8,128)(2,1)S(1)} %get-tuple-element.85), channel_id=1, source_target_pairs={{0,1},{1,2},{2,3},{3,4},{4,5},{5,6},{6,7},{7,8},{8,9},{9,10},{10,1... | collective-permute-start | bytes 57608 | tf_op jit(solution)/shard_map/ppermute | solution.py:16
  98.2 7.2 %collective-permute-start.7 = (bf16[3,25,1,128]{3,1,2,0:T(8,128)(2,1)S(1)}, bf16[3,25,1,128]{3,1,2,0:T(8,128)(2,1)S(1)}, u32[]{:S(2)}, u32[]{:S(2)}) collective-permute-start(bf16[3,25,1,128]{3,1,2,0:T(8,128)(2,1)S(1)} %get-tuple-element.86), channel_id=1, source_target_pairs={{1,0},{2,1},{3,2},{4,3},{5,4},{6,5},{7,6},{8,7},{9,8},{10,9},{11,1... | collective-permute-start | bytes 57608 | tf_op jit(solution)/shard_map/ppermute | solution.py:18
  99.5 6.5 %copy-start.52 = (bf16[3,1,10,128]{3,1,2,0:T(2,128)(2,1)}, bf16[3,1,10,128]{3,1,2,0:T(2,128)(2,1)S(1)}, u32[]{:S(2)}) copy-start(bf16[3,1,10,128]{3,1,2,0:T(2,128)(2,1)S(1)} %collective-permute-done.9) | copy-start | bytes 23044
  100.2 17.5 %collective-permute-start.10 = (bf16[3,25,1,128]{3,1,2,0:T(8,128)(2,1)}, bf16[3,25,1,128]{3,1,2,0:T(8,128)(2,1)}, u32[]{:S(2)}, u32[]{:S(2)}) collective-permute-start(bf16[3,25,1,128]{3,1,2,0:T(8,128)(2,1)} %get-tuple-element.83), channel_id=1, source_target_pairs={{0,1},{1,2},{2,3},{3,4},{4,5},{5,6},{6,7},{7,8},{8,9},{9,10},{10,1... | collective-permute-start | bytes 57608 | tf_op jit(solution)/shard_map/ppermute | solution.py:16
  104.1 13.6 %collective-permute-start.11 = (bf16[3,25,1,128]{3,1,2,0:T(8,128)(2,1)}, bf16[3,25,1,128]{3,1,2,0:T(8,128)(2,1)}, u32[]{:S(2)}, u32[]{:S(2)}) collective-permute-start(bf16[3,25,1,128]{3,1,2,0:T(8,128)(2,1)} %get-tuple-element.84), channel_id=1, source_target_pairs={{1,0},{2,1},{3,2},{4,3},{5,4},{6,5},{7,6},{8,7},{9,8},{10,9},{11,1... | collective-permute-start | bytes 57608 | tf_op jit(solution)/shard_map/ppermute | solution.py:18
  124.1 2.5 copy-start.11
  124.1 3.7 %copy-start.12 = (bf16[690,384]{1,0:T(8,128)(2,1)S(1)}, bf16[690,384]{1,0:T(8,128)(2,1)}, u32[]{:S(2)}) copy-start(bf16[690,384]{1,0:T(8,128)(2,1)} %reshape.154) | copy-start | bytes 1589764
  124.1 3.7 %copy-start.37 = (bf16[1,1,3,128,128]{4,3,2,1,0:T(8,128)(2,1)S(1)}, bf16[1,1,3,128,128]{4,3,2,1,0:T(8,128)(2,1)}, u32[]{:S(2)}) copy-start(bf16[1,1,3,128,128]{4,3,2,1,0:T(8,128)(2,1)} %get-tuple-element.41) | copy-start | bytes 294916
  125.1 3.1 %copy-start.13 = (bf16[690,384]{1,0:T(8,128)(2,1)S(1)}, bf16[690,384]{1,0:T(8,128)(2,1)}, u32[]{:S(2)}) copy-start(bf16[690,384]{1,0:T(8,128)(2,1)} %reshape.155) | copy-start | bytes 1589764
  125.2 3.1 %copy-start.36 = (bf16[1,1,3,128,128]{4,3,2,1,0:T(8,128)(2,1)S(1)}, bf16[1,1,3,128,128]{4,3,2,1,0:T(8,128)(2,1)}, u32[]{:S(2)}) copy-start(bf16[1,1,3,128,128]{4,3,2,1,0:T(8,128)(2,1)} %get-tuple-element.40) | copy-start | bytes 294916
  270.0 3.1 %copy-start.26 = (f32[3,3,3,128,128]{4,3,2,1,0:T(8,128)S(1)}, f32[3,3,3,128,128]{4,3,2,1,0:T(8,128)}, u32[]{:S(2)}) copy-start(f32[3,3,3,128,128]{4,3,2,1,0:T(8,128)} %get-tuple-element.7) | copy-start | bytes 5308420
  (39 other events, 52.8 us)
Sparse Core Ops, SparseCore 0:
  124.3 145.6 all-reduce.7
where the time goes:
time: 283 us; the launch traced here: 281 us
  waiting for transfers between devices  90.6 us (32%)
  local copies, waits for them, and re-layouts  62.4 us (22%)
  blocking collectives  45 us (16%)
  starting transfers between devices  31 us (11%)
  matrix products  24.2 us (9%)
  between operations  15.4 us (5%)
  other arithmetic  12.8 us (5%)
    psum x1, waiting for transfers between devices, body(): lax.psum((grad_one, bias_a, grad_two, bias_b), ('ha', 'wa'))  88.1 us
    psum x1, blocking collectives, body(): lax.psum((grad_one, bias_a, grad_two, bias_b), ('ha', 'wa'))  45 us
    reshape x27, local copies, waits for them, and re-layouts, convolve(): wide[step_t:step_t + frames, step_h:step_h + rows].reshape(-1, 3 * inner)  25.2 us
    slice x30, local copies, waits for them, and re-layouts, convolve(): wide[step_t:step_t + frames, step_h:step_h + rows].reshape(-1, 3 * inner)  25.2 us
    ppermute x6, starting transfers between devices, with_halo(): lax.ppermute(tail, axis, [(i, (i + 1) % count) for i in range(ends)])  23.3 us
    dot_general x27, matrix products, convolve(): jnp.dot(slab, kernel[step_t, step_h].reshape(3 * inner, -1), preferred_el...  17.8 us
    ppermute x6, starting transfers between devices, with_halo(): lax.ppermute(head, axis, [((i + 1) % count, i) for i in range(ends)])  7.74 us
    dot_general x18, matrix products, kernel_terms(): lax.dot_general(slab, grads, (((0,), (0,)), ((), ())), preferred_element_...  6.47 us
  transfers between devices with their start and end apart: 13, of which 2 were waited for; matrix products, arithmetic and copies ran while one was open for 12% of the time, Pallas kernels for 0%

commit v1 on v0

--- a/solution.py
+++ b/solution.py
@@ -104,8 +104,8 @@
     )
     grad_one = kernel_terms(first_wide, inner.reshape(-1, chans), frames, rows)
     bias_a = jnp.sum(inner.astype(jnp.float32), axis=(0, 1, 2))
-    grad_one, bias_a, grad_two, bias_b = lax.psum(
-        (grad_one, bias_a, grad_two, bias_b), ("ha", "wa")
+    grad_one, bias_a, grad_two, bias_b = jax.lax.psum(
+        jax.lax.psum((grad_one, bias_a, grad_two, bias_b), axis_name="wa"), axis_name="ha"
     )
     return (grad_input, grad_one * factor, bias_a * factor, grad_two * factor, bias_b * factor)
 

time: 283 us -> 329 us (1.16)
  waiting for transfers between devices: 90.6 us -> 144 us
  blocking collectives: 45 us -> 34.5 us
  matrix products: 24.2 us -> 29.7 us
  starting transfers between devices: 31 us -> 27.1 us
  local copies, waits for them, and re-layouts: 62.4 us -> 65.9 us
    psum x1 -> x2, waiting for transfers between devices: 88.1 us -> 130 us  [the longest x1 92.5 us: body(): jax.lax.psum((grad_one, bias_a, grad_two, bias_b), axis_name='wa')]
    ppermute x6, waiting for transfers between devices: 2.47 us -> 13.6 us  [with_halo(): lax.ppermute(head, axis, [((i + 1) % count, i) for i in range(ends)])]
    psum x1 -> x2, blocking collectives: 45 us -> 34.5 us  [the longest x1 29.6 us: body(): jax.lax.psum((grad_one, bias_a, grad_two, bias_b), axis_name='wa')]
    dot_general x18, matrix products: 6.47 us -> 12.6 us  [kernel_terms(): lax.dot_general(slab, grads, (((0,), (0,)), ((), ())), preferred_element_...]
    ppermute x6, starting transfers between devices: 23.3 us -> 19.1 us  [with_halo(): lax.ppermute(tail, axis, [(i, (i + 1) % count) for i in range(ends)])]
    slice x30, local copies, waits for them, and re-layouts: 25.2 us -> 29.1 us  [convolve(): wide[step_t:step_t + frames, step_h:step_h + rows].reshape(-1, 3 * inner)]
  transfers between devices with their start and end apart: 13 -> 14, of which waited for: 2 -> 8; matrix products, arithmetic and copies ran while one was open for 12% -> 10% of each run, Pallas kernels for 0% -> 0%
where the time goes in v1:
time: 329 us; the launch traced here: 328 us
  waiting for transfers between devices  144 us (44%)
  local copies, waits for them, and re-layouts  65.9 us (20%)
  blocking collectives  34.5 us (10%)
  matrix products  29.7 us (9%)
  starting transfers between devices  27.1 us (8%)
  between operations  15.3 us (5%)
  other arithmetic  11.3 us (3%)
    psum x1, waiting for transfers between devices, body(): jax.lax.psum((grad_one, bias_a, grad_two, bias_b), axis_name='wa')  92.5 us
    psum x1, waiting for transfers between devices, body(): jax.lax.psum(jax.lax.psum((grad_one, bias_a, grad_two, bias_b), axis_name...  37.6 us
    psum x1, blocking collectives, body(): jax.lax.psum((grad_one, bias_a, grad_two, bias_b), axis_name='wa')  29.6 us
    slice x30, local copies, waits for them, and re-layouts, convolve(): wide[step_t:step_t + frames, step_h:step_h + rows].reshape(-1, 3 * inner)  29.1 us
    reshape x27, local copies, waits for them, and re-layouts, convolve(): wide[step_t:step_t + frames, step_h:step_h + rows].reshape(-1, 3 * inner)  26 us
    ppermute x6, starting transfers between devices, with_halo(): lax.ppermute(tail, axis, [(i, (i + 1) % count) for i in range(ends)])  19.1 us
    dot_general x27, matrix products, convolve(): jnp.dot(slab, kernel[step_t, step_h].reshape(3 * inner, -1), preferred_el...  17.1 us
    ppermute x6, waiting for transfers between devices, with_halo(): lax.ppermute(head, axis, [((i + 1) % count, i) for i in range(ends)])  13.6 us
  transfers between devices with their start and end apart: 14, of which 8 were waited for; matrix products, arithmetic and copies ran while one was open for 10% of the time, Pallas kernels for 0%

profile of v1, /device:TPU:0, one launch (start us, length us, event | category | flops | bytes accessed | tf_op | source)
XLA Modules:
  0.0 327.5 jit_solution(12337049045566607485)
XLA Ops:
  9.2 4.9 %collective-permute-start = (bf16[2,3,1,10,128]{4,2,3,1,0:T(2,128)(2,1)S(1)}, bf16[2,3,1,10,128]{4,2,3,1,0:T(2,128)(2,1)S(1)}, u32[]{:S(2)}, u32[]{:S(2)}) collective-permute-start(bf16[2,3,1,10,128]{4,2,3,1,0:T(2,128)(2,1)S(1)} %get-tuple-element.79), channel_id=1, source_target_pairs={{0,16},{1,17},{2,18},{3,19},{4,20},{5,21},{6,22},{7,23},{8,24},{9,... | collective-permute-start | bytes 46088 | tf_op jit(solution)/shard_map/ppermute | solution.py:16
  14.1 1.3 collective-permute-start.1
  15.4 2.0 copy.18
  18.5 1.4 collective-permute-done.1
  23.5 2.6 collective-permute-done.3
  27.9 2.2 fusion.63
  44.4 1.3 pad_maximum_fusion.1
  45.7 2.5 fusion.62
  68.9 1.5 fusion.72
  70.4 1.4 convolution_add_fusion.15
  76.3 1.3 fusion.71
  77.7 1.6 convolution_add_fusion.23
  84.2 3.1 collective-permute-start.8
  91.6 1.4 collective-permute-done.9
  93.0 3.3 collective-permute-start.10
  96.3 1.3 collective-permute-start.11
  98.0 2.3 collective-permute-done.11
  110.2 1.4 copy.39
  111.7 3.2 collective-permute-start.4
  116.3 4.2 %collective-permute-done.5 = bf16[3,1,10,128]{3,1,2,0:T(2,128)(2,1)S(1)} collective-permute-done((bf16[3,1,10,128]{3,1,2,0:T(2,128)(2,1)S(1)}, bf16[3,1,10,128]{3,1,2,0:T(2,128)(2,1)S(1)}, u32[]{:S(2)}, u32[]{:S(2)}) %collective-permute-start.5) | collective-permute-done | bytes 7712 | tf_op jit(solution)/shard_map/ppermute | solution.py:18
  120.5 3.3 %collective-permute-start.6 = (bf16[3,25,1,128]{3,1,2,0:T(8,128)(2,1)S(1)}, bf16[3,25,1,128]{3,1,2,0:T(8,128)(2,1)S(1)}, u32[]{:S(2)}, u32[]{:S(2)}) collective-permute-start(bf16[3,25,1,128]{3,1,2,0:T(8,128)(2,1)S(1)} %get-tuple-element.89), channel_id=1, source_target_pairs={{0,1},{1,2},{2,3},{3,4},{4,5},{5,6},{6,7},{7,8},{8,9},{9,10},{10,1... | collective-permute-start | bytes 57608 | tf_op jit(solution)/shard_map/ppermute | solution.py:16
  123.8 1.5 collective-permute-start.7
  126.2 1.7 collective-permute-done.7
  128.0 92.5 %all-reduce.11.cloned.1.call-done = (f32[3,3,3,128,128]{4,3,2,1,0:T(8,128)}, f32[3,3,3,128,128]{4,3,2,1,0:T(8,128)}) async-done(((f32[3,3,3,128,128]{4,3,2,1,0:T(8,128)}, f32[3,3,3,128,128]{4,3,2,1,0:T(8,128)}), (f32[3,3,3,128,128]{4,3,2,1,0:T(8,128)}, f32[3,3,3,128,128]{4,3,2,1,0:T(8,128)})) %all-reduce.11.cloned.1.call-update) | async-done | bytes 3538960 | tf_op jit(solution)/shard_map/psum | solution.py:108
  221.0 1.9 fusion.61
  236.6 1.3 fusion.73
  237.9 1.3 convolution_add_fusion.7
  243.1 29.6 %all-reduce.4 = (f32[128]{0:T(128)S(1)}, f32[128]{0:T(128)S(1)}) all-reduce(f32[128]{0:T(128)S(1)} %get-tuple-element.97, f32[128]{0:T(128)S(1)} %get-tuple-element.91), channel_id=1, replica_groups=mesh['ha'=2,'wa'=16] {'wa'}, use_global_device_ids=true, to_apply=%region_3.4 | all-reduce | flops 256 | bytes 2048 | tf_op jit(solution)/shard_map/psum | solution.py:108
  272.7 4.9 %all-reduce.6 = (f32[128]{0:T(128)S(1)}, f32[128]{0:T(128)S(1)}) all-reduce(f32[128]{0:T(128)S(1)} %get-tuple-element.5, f32[128]{0:T(128)S(1)} %get-tuple-element.6), channel_id=1, replica_groups=mesh['ha'=2,'wa'=16] {'ha'}, use_global_device_ids=true, to_apply=%region_4.5 | all-reduce | flops 256 | bytes 2048 | tf_op jit(solution)/shard_map/psum | solution.py:107
  278.7 37.6 %all-reduce.13.cloned.1.call-done = (f32[3,3,3,128,128]{4,3,2,1,0:T(8,128)}, f32[3,3,3,128,128]{4,3,2,1,0:T(8,128)}) async-done(((f32[3,3,3,128,128]{4,3,2,1,0:T(8,128)}, f32[3,3,3,128,128]{4,3,2,1,0:T(8,128)}), (f32[3,3,3,128,128]{4,3,2,1,0:T(8,128)}, f32[3,3,3,128,128]{4,3,2,1,0:T(8,128)})) %all-reduce.13.cloned.1.call-update) | async-done | bytes 3538960 | tf_op jit(solution)/shard_map/psum | solution.py:107
  316.2 3.1 broadcast_multiply_fusion
  319.3 1.4 broadcast_multiply_fusion.1
  (250 shorter events, 87.9 us)
Async XLA Ops:
  7.2 213.4 %all-reduce.11.cloned.1.call-start = ((), (), s32[]{:S(2)}) async-start(), calls=%async_computation | async-start | bytes 7077888 | tf_op jit(solution)/shard_map/psum | solution.py:108
  9.2 9.3 %collective-permute-start = (bf16[2,3,1,10,128]{4,2,3,1,0:T(2,128)(2,1)S(1)}, bf16[2,3,1,10,128]{4,2,3,1,0:T(2,128)(2,1)S(1)}, u32[]{:S(2)}, u32[]{:S(2)}) collective-permute-start(bf16[2,3,1,10,128]{4,2,3,1,0:T(2,128)(2,1)S(1)} %get-tuple-element.79), channel_id=1, source_target_pairs={{0,16},{1,17},{2,18},{3,19},{4,20},{5,21},{6,22},{7,23},{8,24},{9,... | collective-permute-start | bytes 46088 | tf_op jit(solution)/shard_map/ppermute | solution.py:16
  14.1 5.8 %collective-permute-start.1 = (bf16[2,3,1,10,128]{4,2,3,1,0:T(2,128)(2,1)S(1)}, bf16[2,3,1,10,128]{4,2,3,1,0:T(2,128)(2,1)S(1)}, u32[]{:S(2)}, u32[]{:S(2)}) collective-permute-start(bf16[2,3,1,10,128]{4,2,3,1,0:T(2,128)(2,1)S(1)} %get-tuple-element.80), channel_id=1, source_target_pairs={{16,0},{17,1},{18,2},{19,3},{20,4},{21,5},{22,6},{23,7},{24,8},{25... | collective-permute-start | bytes 46088 | tf_op jit(solution)/shard_map/ppermute | solution.py:18
  17.4 5.1 %copy-start = (bf16[3,3,3,128,128]{4,3,2,1,0:T(8,128)(2,1)S(1)}, bf16[3,3,3,128,128]{4,3,2,1,0:T(8,128)(2,1)}, u32[]{:S(2)}) copy-start(bf16[3,3,3,128,128]{4,3,2,1,0:T(8,128)(2,1)} %param.11) | copy-start | bytes 2654212
  19.9 3.5 %collective-permute-start.2 = (bf16[2,3,25,1,128]{4,2,3,1,0:T(8,128)(2,1)S(1)}, bf16[2,3,25,1,128]{4,2,3,1,0:T(8,128)(2,1)S(1)}, u32[]{:S(2)}, u32[]{:S(2)}) collective-permute-start(bf16[2,3,25,1,128]{4,2,3,1,0:T(8,128)(2,1)S(1)} %get-tuple-element.77), channel_id=1, source_target_pairs={{0,1},{1,2},{2,3},{3,4},{4,5},{5,6},{6,7},{7,8},{8,9},{9,10},{10,1... | collective-permute-start | bytes 115208 | tf_op jit(solution)/shard_map/ppermute | solution.py:16
  21.2 4.8 %collective-permute-start.3 = (bf16[2,3,25,1,128]{4,2,3,1,0:T(8,128)(2,1)S(1)}, bf16[2,3,25,1,128]{4,2,3,1,0:T(8,128)(2,1)S(1)}, u32[]{:S(2)}, u32[]{:S(2)}) collective-permute-start(bf16[2,3,25,1,128]{4,2,3,1,0:T(8,128)(2,1)S(1)} %get-tuple-element.78), channel_id=1, source_target_pairs={{1,0},{2,1},{3,2},{4,3},{5,4},{6,5},{7,6},{8,7},{9,8},{10,9},{11,1... | collective-permute-start | bytes 115208 | tf_op jit(solution)/shard_map/ppermute | solution.py:18
  65.6 3.2 copy-start.45
  66.6 3.7 %copy-start.44 = (bf16[1,1,3,128,128]{4,3,2,1,0:T(8,128)(2,1)S(1)}, bf16[1,1,3,128,128]{4,3,2,1,0:T(8,128)(2,1)}, u32[]{:S(2)}) copy-start(bf16[1,1,3,128,128]{4,3,2,1,0:T(8,128)(2,1)} %get-tuple-element.56) | copy-start | bytes 294916
  67.8 4.0 %copy-start.43 = (bf16[1,1,3,128,128]{4,3,2,1,0:T(8,128)(2,1)S(1)}, bf16[1,1,3,128,128]{4,3,2,1,0:T(8,128)(2,1)}, u32[]{:S(2)}) copy-start(bf16[1,1,3,128,128]{4,3,2,1,0:T(8,128)(2,1)} %get-tuple-element.55) | copy-start | bytes 294916
  68.9 3.0 copy-start.9
  68.9 3.4 %copy-start.10 = (bf16[690,384]{1,0:T(8,128)(2,1)S(1)}, bf16[690,384]{1,0:T(8,128)(2,1)}, u32[]{:S(2)}) copy-start(bf16[690,384]{1,0:T(8,128)(2,1)} %reshape.144) | copy-start | bytes 1589764
  68.9 3.4 %copy-start.42 = (bf16[1,1,3,128,128]{4,3,2,1,0:T(8,128)(2,1)S(1)}, bf16[1,1,3,128,128]{4,3,2,1,0:T(8,128)(2,1)}, u32[]{:S(2)}) copy-start(bf16[1,1,3,128,128]{4,3,2,1,0:T(8,128)(2,1)} %get-tuple-element.54) | copy-start | bytes 294916
  75.2 4.1 %copy-start.36 = (bf16[1,1,3,128,128]{4,3,2,1,0:T(8,128)(2,1)S(1)}, bf16[1,1,3,128,128]{4,3,2,1,0:T(8,128)(2,1)}, u32[]{:S(2)}) copy-start(bf16[1,1,3,128,128]{4,3,2,1,0:T(8,128)(2,1)} %get-tuple-element.64) | copy-start | bytes 294916
  76.3 3.0 copy-start.3
  76.3 3.4 %copy-start.4 = (bf16[690,384]{1,0:T(8,128)(2,1)S(1)}, bf16[690,384]{1,0:T(8,128)(2,1)}, u32[]{:S(2)}) copy-start(bf16[690,384]{1,0:T(8,128)(2,1)} %reshape.134) | copy-start | bytes 1589764
  76.3 3.4 %copy-start.35 = (bf16[1,1,3,128,128]{4,3,2,1,0:T(8,128)(2,1)S(1)}, bf16[1,1,3,128,128]{4,3,2,1,0:T(8,128)(2,1)}, u32[]{:S(2)}) copy-start(bf16[1,1,3,128,128]{4,3,2,1,0:T(8,128)(2,1)} %get-tuple-element.63) | copy-start | bytes 294916
  84.2 13.4 %copy-start.24 = (bf16[3,23,10,128]{3,1,2,0:T(8,128)(2,1)}, bf16[3,23,10,128]{3,1,2,0:T(8,128)(2,1)S(1)}, u32[]{:S(2)}) copy-start(bf16[3,23,10,128]{3,1,2,0:T(8,128)(2,1)S(1)} %get-tuple-element.70) | copy-start | bytes 529924
  84.2 7.4 %collective-permute-start.8 = (bf16[3,1,10,128]{3,1,2,0:T(2,128)(2,1)S(1)}, bf16[3,1,10,128]{3,1,2,0:T(2,128)(2,1)S(1)}, u32[]{:S(2)}, u32[]{:S(2)}) collective-permute-start(bf16[3,1,10,128]{3,1,2,0:T(2,128)(2,1)S(1)} %get-tuple-element.93), channel_id=1, source_target_pairs={{0,16},{1,17},{2,18},{3,19},{4,20},{5,21},{6,22},{7,23},{8,24},{9,... | collective-permute-start | bytes 23048 | tf_op jit(solution)/shard_map/ppermute | solution.py:16
  87.4 5.6 %collective-permute-start.9 = (bf16[3,1,10,128]{3,1,2,0:T(2,128)(2,1)S(1)}, bf16[3,1,10,128]{3,1,2,0:T(2,128)(2,1)S(1)}, u32[]{:S(2)}, u32[]{:S(2)}) collective-permute-start(bf16[3,1,10,128]{3,1,2,0:T(2,128)(2,1)S(1)} %get-tuple-element.94), channel_id=1, source_target_pairs={{16,0},{17,1},{18,2},{19,3},{20,4},{21,5},{22,6},{23,7},{24,8},{25... | collective-permute-start | bytes 23048 | tf_op jit(solution)/shard_map/ppermute | solution.py:18
  93.0 5.0 %collective-permute-start.10 = (bf16[3,25,1,128]{3,1,2,0:T(8,128)(2,1)S(1)}, bf16[3,25,1,128]{3,1,2,0:T(8,128)(2,1)S(1)}, u32[]{:S(2)}, u32[]{:S(2)}) collective-permute-start(bf16[3,25,1,128]{3,1,2,0:T(8,128)(2,1)S(1)} %get-tuple-element.87), channel_id=1, source_target_pairs={{0,1},{1,2},{2,3},{3,4},{4,5},{5,6},{6,7},{7,8},{8,9},{9,10},{10,1... | collective-permute-start | bytes 57608 | tf_op jit(solution)/shard_map/ppermute | solution.py:16
  96.3 4.0 %collective-permute-start.11 = (bf16[3,25,1,128]{3,1,2,0:T(8,128)(2,1)S(1)}, bf16[3,25,1,128]{3,1,2,0:T(8,128)(2,1)S(1)}, u32[]{:S(2)}, u32[]{:S(2)}) collective-permute-start(bf16[3,25,1,128]{3,1,2,0:T(8,128)(2,1)S(1)} %get-tuple-element.88), channel_id=1, source_target_pairs={{1,0},{2,1},{3,2},{4,3},{5,4},{6,5},{7,6},{8,7},{9,8},{10,9},{11,1... | collective-permute-start | bytes 57608 | tf_op jit(solution)/shard_map/ppermute | solution.py:18
  97.9 2.9 copy-start.27
  110.2 206.0 %all-reduce.13.cloned.1.call-start = ((), (), s32[]{:S(2)}) async-start(), calls=%async_computation.1 | async-start | bytes 7077888 | tf_op jit(solution)/shard_map/psum | solution.py:107
  111.7 4.6 %collective-permute-start.4 = (bf16[3,1,10,128]{3,1,2,0:T(2,128)(2,1)S(1)}, bf16[3,1,10,128]{3,1,2,0:T(2,128)(2,1)S(1)}, u32[]{:S(2)}, u32[]{:S(2)}) collective-permute-start(bf16[3,1,10,128]{3,1,2,0:T(2,128)(2,1)S(1)} %get-tuple-element.95), channel_id=1, source_target_pairs={{0,16},{1,17},{2,18},{3,19},{4,20},{5,21},{6,22},{7,23},{8,24},{9,... | collective-permute-start | bytes 23048 | tf_op jit(solution)/shard_map/ppermute | solution.py:16
  114.8 5.6 %collective-permute-start.5 = (bf16[3,1,10,128]{3,1,2,0:T(2,128)(2,1)S(1)}, bf16[3,1,10,128]{3,1,2,0:T(2,128)(2,1)S(1)}, u32[]{:S(2)}, u32[]{:S(2)}) collective-permute-start(bf16[3,1,10,128]{3,1,2,0:T(2,128)(2,1)S(1)} %get-tuple-element.96), channel_id=1, source_target_pairs={{16,0},{17,1},{18,2},{19,3},{20,4},{21,5},{22,6},{23,7},{24,8},{25... | collective-permute-start | bytes 23048 | tf_op jit(solution)/shard_map/ppermute | solution.py:18
  120.5 5.7 %collective-permute-start.6 = (bf16[3,25,1,128]{3,1,2,0:T(8,128)(2,1)S(1)}, bf16[3,25,1,128]{3,1,2,0:T(8,128)(2,1)S(1)}, u32[]{:S(2)}, u32[]{:S(2)}) collective-permute-start(bf16[3,25,1,128]{3,1,2,0:T(8,128)(2,1)S(1)} %get-tuple-element.89), channel_id=1, source_target_pairs={{0,1},{1,2},{2,3},{3,4},{4,5},{5,6},{6,7},{7,8},{8,9},{9,10},{10,1... | collective-permute-start | bytes 57608 | tf_op jit(solution)/shard_map/ppermute | solution.py:16
  123.8 4.0 %collective-permute-start.7 = (bf16[3,25,1,128]{3,1,2,0:T(8,128)(2,1)S(1)}, bf16[3,25,1,128]{3,1,2,0:T(8,128)(2,1)S(1)}, u32[]{:S(2)}, u32[]{:S(2)}) collective-permute-start(bf16[3,25,1,128]{3,1,2,0:T(8,128)(2,1)S(1)} %get-tuple-element.90), channel_id=1, source_target_pairs={{1,0},{2,1},{3,2},{4,3},{5,4},{6,5},{7,6},{8,7},{9,8},{10,9},{11,1... | collective-permute-start | bytes 57608 | tf_op jit(solution)/shard_map/ppermute | solution.py:18
  235.6 3.6 %copy-start.18 = (bf16[690,384]{1,0:T(8,128)(2,1)S(1)}, bf16[690,384]{1,0:T(8,128)(2,1)}, u32[]{:S(2)}) copy-start(bf16[690,384]{1,0:T(8,128)(2,1)} %reshape.153) | copy-start | bytes 1589764
  236.6 2.7 copy-start.50
  236.6 3.0 copy-start.19
  236.6 3.0 copy-start.49
  316.2 3.1 copy-start.26
  (39 other events, 56.5 us)
Sparse Core Ops, SparseCore 0:
  110.3 110.1 all-reduce.10
  222.9 93.2 all-reduce.12
